TPU v7x, 256 devices: a whole 4x4x8 slice. The times are simulated.
256 devices in a mesh: blk: 32 (over z, y_lo, core), axial: 8 (over x, y_hi).
Axes of the slice: x: 4, y: 4 (y_hi: 2, y_lo: 2; y = y_hi * 2 + y_lo), z: 8, core: 2. Of those that a mesh axis runs over, the one named last changes fastest.
Arguments:
- fields: float32 [5, 48, 256, 1024], P(None, None, 'blk', 'axial'), may hold values from -6 to 6
- inv_volume: float32 [48, 256, 1024], P(None, 'blk', 'axial'), may hold values from 0.5 to 2
- radius_ratio: float32 [48, 256, 1024], P(None, 'blk', 'axial'), may hold values from 58.09475 to 172.6007
- time_step: float32 [48, 256, 1024], P(None, 'blk', 'axial'), may hold values from 8 to 32
- jac_circ: float32 [5, 5], replicated, may hold values from -2.4 to 2.4
- jac_other: float32 [2, 5, 5], replicated, may hold values from -2.4 to 2.4
Outputs:
- advanced: float32 [5, 48, 256, 1024], P(None, None, 'blk', 'axial')
All inputs are finite; a program needn't handle non-finite values.
Results may differ from a plain program's by a relative error of at most 0.0003.
Values sent between devices are 32-bit elements; how exact they have to be, the bound alone decides.
A program may use at most 64 MiB of HBM per device.

v0:
```python
import functools

import jax
import jax.numpy as jnp
from jax import lax
from jax.experimental import pallas as pl
from jax.experimental.pallas import tpu as pltpu
from jax.sharding import Mesh
from jax.sharding import PartitionSpec as P

BLK = ("blk_0", "blk_1", "blk_2")
DISSIPATION = 0.03125
SECTION_ONE = 0.6
COURANT_RATIO = 2.0
SCALING_POWER = 2.0 / 3.0

NV = 5
TILES = 6
HALF = 3
ROWS = 8
SUB = 8
LANES = 128
UNITS = HALF * NV
F32 = jnp.float32


def kernel(
    nz,
    na,
    fields,
    inv_volume,
    radius_ratio,
    time_step,
    jac_c,
    jac_o,
    out,
    u1,
    u2,
    vol,
    rad,
    dt,
    wgt,
    cc,
    cp,
    yy,
    qrow,
    qhalo,
    pk,
    pkh,
    pb,
    pr,
    mb,
    rb,
    xb,
    xr,
    xx,
    gg,
    gr,
    gm,
    gt,
    td,
    tp,
    tx,
    res,
    in_sem,
    out_sem,
    circ_s,
    circ_r,
    ax_s,
    ax_r,
    q_s,
    q_r,
    gp_s,
    gp_r,
    ga_s,
    ga_r,
    pp_s,
    pp_r,
    pa_s,
    pa_r,
    xa_s,
    xa_r,
    xp_s,
    xp_r,
):
    ranks = nz * 2
    z = lax.axis_index("blk_0")
    y = lax.axis_index("blk_1")
    c = lax.axis_index("blk_2")
    a = lax.axis_index("axial")
    me = z * 2 + y

    def blk_device(b):
        return {"blk_0": b // 4, "blk_1": (b // 2) % 2, "blk_2": b % 2, "axial": a}

    def ax_device(index):
        return {"blk_0": z, "blk_1": y, "blk_2": c, "axial": index}

    def rank_device(rank):
        return {"blk_0": rank // 2, "blk_1": rank % 2, "blk_2": c, "axial": a}

    b = me * 2 + c
    size = ranks * 2
    right = blk_device((b + 1) % size)
    left = blk_device((b + size - 1) % size)
    ax_up = ax_device((a + 1) % na)
    ax_down = ax_device((a + na - 1) % na)
    partner = {"blk_0": z, "blk_1": y, "blk_2": 1 - c, "axial": a}
    hops = [dz for k in range(nz // 2, 0, -1) for dz in dict.fromkeys((k, nz - k))] + [0]
    offsets = [(dz, dy) for dz in hops for dy in (1, 0) if (dz, dy) != (0, 0)]

    def peer(n):
        dz, dy = offsets[n]
        return ((z + dz) % nz) * 2 + (y + dy) % 2

    def source(n):
        dz, dy = offsets[n]
        return ((z + nz - dz) % nz) * 2 + (y + dy) % 2

    def remote(src, dst, ssem, rsem, device):
        return pltpu.make_async_remote_copy(
            src_ref=src,
            dst_ref=dst,
            send_sem=ssem,
            recv_sem=rsem,
            device_id=device,
            device_id_type=pl.DeviceIdType.MESH,
        )

    loads = {
        "rad": [pltpu.make_async_copy(radius_ratio.at[:, i, :], rad.at[i + 1], in_sem.at[0, i]) for i in range(ROWS)],
        "vol": [pltpu.make_async_copy(inv_volume.at[:, i, :], vol.at[i], in_sem.at[1, i]) for i in range(ROWS)],
        "u": [pltpu.make_async_copy(fields.at[:, :, i, :], u1.at[:, i + 2], in_sem.at[2, i]) for i in range(ROWS)],
        "dt": [pltpu.make_async_copy(time_step.at[:, i, :], dt.at[i + 2], in_sem.at[3, i]) for i in range(ROWS)],
    }
    for name in ("u", "rad", "vol", "dt"):
        for copy in loads[name]:
            copy.start()

    barrier = pltpu.get_barrier_semaphore()
    greet = [left, right, ax_up, ax_down, partner] + [rank_device(peer(n)) for n in range(len(offsets))]
    for device in greet:
        pl.semaphore_signal(barrier, inc=1, device_id=device, device_id_type=pl.DeviceIdType.MESH)

    lane = lax.broadcasted_iota(jnp.int32, (SUB, LANES), 1)
    sub = lax.broadcasted_iota(jnp.int32, (SUB, LANES), 0)
    core0 = jnp.broadcast_to(c == 0, (SUB, LANES))

    def tile(t):
        return pl.ds(pl.multiple_of(t * SUB, SUB), SUB)

    def inverse_smoothing(ratio):
        scaled = COURANT_RATIO * (1.0 + jnp.exp(SCALING_POWER * jnp.log(ratio)))
        return 1.0 / (0.25 * (scaled * scaled - 1.0))

    def pack(u, t, slot):
        for half in range(2):
            packed = jnp.zeros((SUB, LANES), F32)
            for n in range(NV * ROWS // 2):
                flat = half * (NV * ROWS // 2) + n
                moved = pltpu.roll(u[flat // ROWS, flat % ROWS + 2, tile(t)], 4 * n + 2, 1)
                packed = jnp.where(lane // 4 == n, moved, packed)
            pk[slot, t, half] = packed

    for copy in loads["u"]:
        copy.wait()

    def pack_step(t, carry):
        pack(u1, t, 0)
        return carry

    lax.fori_loop(0, TILES, pack_step, 0)
    pl.semaphore_wait(barrier, len(greet))

    def circ_pair(ref, which, low, high, width, axis):
        def part(start):
            return ref.at[:, pl.ds(start, width)] if axis == 1 else ref.at[pl.ds(start, width)]

        count = ROWS
        to_left = remote(part(low), part(low + count), circ_s.at[which, 0], circ_r.at[which, 0], left)
        to_right = remote(part(low + count - width), part(low - width), circ_s.at[which, 1], circ_r.at[which, 1], right)
        return [to_left, to_right]

    def axial_pair(slot):
        up = remote(pk.at[slot], pkh.at[slot, 0], ax_s.at[slot, 0], ax_r.at[slot, 0], ax_up)
        down = remote(pk.at[slot], pkh.at[slot, 1], ax_s.at[slot, 1], ax_r.at[slot, 1], ax_down)
        return [up, down]

    pending = []

    def begin(copies):
        for copy in copies:
            copy.start()
        pending.extend(copies)
        return copies

    u_halo = begin(circ_pair(u1, 0, 2, 2, 2, 1))
    ax_halo = begin(axial_pair(0))
    for copy in loads["rad"] + loads["vol"]:
        copy.wait()

    def factor_step(t, carry):
        ratio = jnp.zeros((SUB, LANES), F32)
        product = jnp.ones((SUB, LANES), F32)
        first = jnp.zeros((SUB, LANES), F32)
        for i in range(ROWS):
            inverse = inverse_smoothing(rad[i + 1, tile(t)])
            wgt[i, tile(t)] = -vol[i, tile(t)] * inverse
            ratio = 1.0 / (2.0 + inverse - ratio)
            cc[i, tile(t)] = ratio
            previous = product
            product = product * ratio
            cp[i, tile(t)] = product
            first = first + previous * product
        gg[t, 0] = first
        gg[t, 1] = product
        gg[t, 2] = ratio
        return carry

    lax.fori_loop(0, TILES, factor_step, 0)
    other = 3 * (1 - c)
    mine = 3 * c
    g_pair = begin([remote(gg.at[pl.ds(other, HALF)], gr, gp_s, gp_r, partner)])
    for copy in loads["dt"]:
        copy.wait()
    rad_halo = begin(circ_pair(rad, 1, 1, 1, 1, 0))
    dt_halo = begin(circ_pair(dt, 2, 2, 2, 2, 0))

    def by_core(own, theirs):
        return jnp.where(core0, own, theirs), jnp.where(core0, theirs, own)

    def join(a_first, a_cross, a_last, b_first, b_cross, b_last):
        d = 1.0 / (1.0 - a_last * b_first)
        return (
            d,
            a_first + a_cross * a_cross * d * b_first,
            a_cross * d * b_cross,
            b_last + b_cross * b_cross * d * a_last,
        )

    def inner_pair(alpha, beta, a_last, b_first, d):
        return d * (alpha + a_last * beta), d * (beta + b_first * alpha)

    g_pair[0].wait_recv()

    def merge_step(t, carry):
        pairs = [by_core(gg[mine + t, n], gr[t, n]) for n in range(3)]
        (a_first, b_first), (a_cross, b_cross), (a_last, b_last) = pairs
        d, first, cross, last = join(a_first, a_cross, a_last, b_first, b_cross, b_last)
        for n, value in enumerate((a_cross, a_last, b_first, b_cross, d)):
            gm[1, t, n] = value
        for n, value in enumerate((first, cross, last)):
            gm[0, t, n] = value
        return carry

    lax.fori_loop(0, HALF, merge_step, 0)

    def spread(src_of, dst, ssem, rsem):
        for n in range(len(offsets)):
            target = peer(n)

            @pl.when(target < UNITS)
            def _(n=n, target=target):
                remote(src_of(target), dst.at[me], ssem.at[n], rsem.at[me], rank_device(target)).start()

    def spread_end(src_of, dst, ssem, rsem):
        for n in range(len(offsets)):
            target = peer(n)

            @pl.when(target < UNITS)
            def _(n=n, target=target):
                remote(src_of(target), dst.at[me], ssem.at[n], rsem.at[me], rank_device(target)).wait_send()

    def spread_recv(dst, rsem):
        for n in range(len(offsets)):
            origin = source(n)
            remote(dst.at[origin], dst.at[origin], rsem.at[origin], rsem.at[origin], rank_device(origin)).wait_recv()

    def g_source(target):
        return gm.at[0, target // NV, pl.ds(0, 3)]

    spread(g_source, gt, ga_s, ga_r)
    for copy in u_halo + ax_halo:
        copy.wait_recv()

    def splat(value):
        return jnp.broadcast_to(value, (SUB, LANES))

    def residual_step(u, slot, t, carry):
        edges = []
        low_edge = jnp.broadcast_to(a == 0, (SUB, LANES))
        high_edge = jnp.broadcast_to(a == na - 1, (SUB, LANES))
        for half in range(2):
            from_low = jnp.where(low_edge, 0.0, pkh[slot, 0, t, half])
            from_high = jnp.where(high_edge, 0.0, pkh[slot, 1, t, half])
            edges.append(jnp.where(lane % 4 < 2, from_low, from_high))
        above = jnp.minimum(t * SUB + SUB, TILES * SUB - 1)
        below = jnp.maximum(t * SUB - 1, 0)
        ahead = [jnp.zeros((SUB, LANES), F32)] * NV
        start = [jnp.zeros((SUB, LANES), F32)] * NV
        product = jnp.ones((SUB, LANES), F32)
        for i in range(ROWS):
            total = [None] * NV
            for m in range(NV):
                centre = u[m, i + 2, tile(t)]
                circ = (2.0 / 3.0) * (u[m, i + 3, tile(t)] - u[m, i + 1, tile(t)]) - (1.0 / 12.0) * (
                    u[m, i + 4, tile(t)] - u[m, i, tile(t)]
                )
                flat = m * ROWS + i
                half, n = flat // (NV * ROWS // 2), flat % (NV * ROWS // 2)
                edge = pltpu.roll(edges[half], LANES - (4 * n + 2), 1)
                plus1 = pltpu.roll(jnp.where(lane < 1, edge, centre), LANES - 1, 1)
                plus2 = pltpu.roll(jnp.where(lane < 2, edge, centre), LANES - 2, 1)
                minus1 = pltpu.roll(jnp.where(lane > LANES - 2, edge, centre), 1, 1)
                minus2 = pltpu.roll(jnp.where(lane > LANES - 3, edge, centre), 2, 1)
                axial = plus1 - minus1
                fourth = (plus2 + minus2) - 4.0 * (plus1 + minus1) + 6.0 * centre
                over = jnp.where(
                    sub == SUB - 1, splat(u[m, i + 2, pl.ds(above, 1)]), pltpu.roll(centre, SUB - 1, 0)
                )
                under = jnp.where(sub == 0, splat(u[m, i + 2, pl.ds(below, 1)]), pltpu.roll(centre, 1, 0))
                normal = over - under
                for v in range(NV):
                    term = jac_c[v, m] * circ + (0.5 * jac_o[0, v, m]) * axial + (0.5 * jac_o[1, v, m]) * normal
                    if v == m:
                        term = term + DISSIPATION * fourth
                    total[v] = term if total[v] is None else total[v] + term
            weight = wgt[i, tile(t)]
            ratio = cc[i, tile(t)]
            for v in range(NV):
                scaled = weight * total[v]
                if slot == 0 and i == 0:
                    qrow[0, v, tile(t)] = scaled
                if slot == 0 and i == ROWS - 1:
                    qrow[1, v, tile(t)] = scaled
                ahead[v] = (scaled + ahead[v]) * ratio
                yy[v, i, tile(t)] = ahead[v]
                start[v] = start[v] + product * ahead[v]
            product = cp[i, tile(t)]
        for v in range(NV):
            pb[slot, t, v, 0] = start[v]
            pb[slot, t, v, 1] = ahead[v]
        return carry

    def tree_factors():
        for r in range(ranks):
            for n in range(3):
                td[r, n] = gt[r, n]
        first, width, node = 0, ranks, ranks
        while width > 1:
            for k in range(0, width, 2):
                left_node, right_node = first + k, first + k + 1
                d, g0, g1, g2 = join(*(td[left_node, n] for n in range(3)), *(td[right_node, n] for n in range(3)))
                for n, value in enumerate((g0, g1, g2, d)):
                    td[node, n] = value
                node += 1
            first, width = first + width, width // 2
        top = 2 * ranks - 2
        inner = 1.0 - td[top, 1]
        td[top + 1, 0] = 1.0 / (inner * inner - td[top, 0] * td[top, 2])

    def tree_solve(slot):
        levels = []
        first, width, node = 0, ranks, ranks
        for r in range(ranks):
            for n in range(2):
                tp[r, n] = rb[slot, r, n]
        while width > 1:
            for k in range(0, width, 2):
                ln, rn = first + k, first + k + 1
                a0, b0 = inner_pair(tp[ln, 1], tp[rn, 0], td[ln, 2], td[rn, 0], td[node, 3])
                tp[node, 0] = tp[ln, 0] + td[ln, 1] * b0
                tp[node, 1] = tp[rn, 1] + td[rn, 1] * a0
                levels.append((node, ln, rn))
                node += 1
            first, width = first + width, width // 2
        top = 2 * ranks - 2
        inner = 1.0 - td[top, 1]
        det = td[top + 1, 0]
        tx[top, 0] = (inner * tp[top, 1] + td[top, 2] * tp[top, 0]) * det
        tx[top, 1] = (inner * tp[top, 0] + td[top, 0] * tp[top, 1]) * det
        for node, ln, rn in levels[::-1]:
            xl, xh = tx[node, 0], tx[node, 1]
            alpha = tp[ln, 1] + td[ln, 1] * xl
            beta = tp[rn, 0] + td[rn, 1] * xh
            mid_a, mid_b = inner_pair(alpha, beta, td[ln, 2], td[rn, 0], td[node, 3])
            tx[ln, 0] = xl
            tx[ln, 1] = mid_b
            tx[rn, 0] = mid_a
            tx[rn, 1] = xh
        for r in range(ranks):
            for n in range(2):
                xb[slot, r, n] = tx[r, n]

    def section(slot, u):
        lax.fori_loop(0, TILES, functools.partial(residual_step, u, slot), 0)
        pair = begin([remote(pb.at[slot, pl.ds(other, HALF)], pr.at[slot], pp_s.at[slot], pp_r.at[slot], partner)])
        pair[0].wait_recv()

        def merge(t, carry):
            a_cross, a_last, b_first, b_cross, d = (gm[1, t, n] for n in range(5))
            for v in range(NV):
                a_head, b_head = by_core(pb[slot, mine + t, v, 0], pr[slot, t, v, 0])
                a_tail, b_tail = by_core(pb[slot, mine + t, v, 1], pr[slot, t, v, 1])
                a0, b0 = inner_pair(a_tail, b_head, a_last, b_first, d)
                mb[slot, t * NV + v, 0] = a_head + a_cross * b0
                mb[slot, t * NV + v, 1] = b_tail + b_cross * a0
            return carry

        lax.fori_loop(0, HALF, merge, 0)
        spread(lambda target: mb.at[slot, target], rb.at[slot], pa_s.at[slot], pa_r.at[slot])

        q_halo = []
        if slot == 0:
            q_halo = begin(
                [
                    remote(qrow.at[0], qhalo.at[1], q_s.at[0], q_r.at[0], left),
                    remote(qrow.at[1], qhalo.at[0], q_s.at[1], q_r.at[1], right),
                ]
            )

        @pl.when(me < UNITS)
        def _():
            if slot == 0:
                gt[me] = gm[0, me // NV, pl.ds(0, 3)]
                spread_recv(gt, ga_r)
                tree_factors()
            rb[slot, me] = mb[slot, me]
            spread_recv(rb.at[slot], pa_r.at[slot])
            tree_solve(slot)
            xr[slot, me] = xb[slot, me]
            for n in range(len(offsets)):
                remote(
                    xb.at[slot, peer(n)], xr.at[slot, me], xa_s.at[slot, n], xa_r.at[slot, me], rank_device(peer(n))
                ).start()

        for n in range(len(offsets)):
            origin = source(n)

            @pl.when(origin < UNITS)
            def _(origin=origin):
                remote(
                    xr.at[slot, origin], xr.at[slot, origin], xa_r.at[slot, origin], xa_r.at[slot, origin], rank_device(origin)
                ).wait_recv()

        def unmerge(t, carry):
            a_cross, a_last, b_first, b_cross, d = (gm[1, t, n] for n in range(5))
            for v in range(NV):
                xl, xh = xr[slot, t * NV + v, 0], xr[slot, t * NV + v, 1]
                _, b_head = by_core(pb[slot, mine + t, v, 0], pr[slot, t, v, 0])
                a_tail, _ = by_core(pb[slot, mine + t, v, 1], pr[slot, t, v, 1])
                mid_a, mid_b = inner_pair(a_tail + a_cross * xl, b_head + b_cross * xh, a_last, b_first, d)
                xx[slot, mine + t, v, 0] = jnp.where(core0, xl, mid_a)
                xx[slot, mine + t, v, 1] = jnp.where(core0, mid_b, xh)
                res[slot, t, v, 0] = jnp.where(core0, mid_a, xl)
                res[slot, t, v, 1] = jnp.where(core0, xh, mid_b)
            return carry

        lax.fori_loop(0, HALF, unmerge, 0)
        back = begin(
            [remote(res.at[slot], xx.at[slot, pl.ds(mine, HALF)], xp_s.at[slot], xp_r.at[slot], partner)]
        )
        arrival = remote(res.at[slot], xx.at[slot, pl.ds(other, HALF)], xp_s.at[slot], xp_r.at[slot], partner)
        arrival.wait_recv()
        for copy in q_halo:
            copy.wait_recv()

    def sweep(slot, t, v):
        low, high = xx[slot, t, v, 0], xx[slot, t, v, 1]
        values = [None] * ROWS
        later = high
        for i in range(ROWS - 1, -1, -1):
            later = yy[v, i, tile(t)] + cp[i, tile(t)] * low + cc[i, tile(t)] * later
            values[i] = later
        return low, high, values

    section(0, u1)
    for copy in rad_halo + dt_halo:
        copy.wait_recv()

    def update_one(t, carry):
        diag_low = 2.0 + inverse_smoothing(rad[0, tile(t)])
        diag_high = 2.0 + inverse_smoothing(rad[ROWS + 1, tile(t)])
        for v in range(NV):
            low, high, values = sweep(0, t, v)
            low2 = diag_low * low - values[0] - qhalo[0, v, tile(t)]
            high2 = diag_high * high - values[ROWS - 1] - qhalo[1, v, tile(t)]
            for i, value in enumerate([low2, low] + values + [high, high2]):
                u2[v, i, tile(t)] = u1[v, i, tile(t)] + SECTION_ONE * dt[i, tile(t)] * value
        pack(u2, t, 1)
        return carry

    lax.fori_loop(0, TILES, update_one, 0)
    ax_halo = begin(axial_pair(1))
    for copy in ax_halo:
        copy.wait_recv()
    section(1, u2)

    def update_two(t, carry):
        for v in range(NV):
            _, _, values = sweep(1, t, v)
            for i, value in enumerate(values):
                u2[v, i + 2, tile(t)] = u1[v, i + 2, tile(t)] + dt[i + 2, tile(t)] * value
        return carry

    lax.fori_loop(0, TILES, update_two, 0)
    stores = [pltpu.make_async_copy(u2.at[:, i + 2], out.at[:, :, i, :], out_sem.at[i]) for i in range(ROWS)]
    for copy in stores:
        copy.start()
    for copy in pending:
        copy.wait_send()
    spread_end(g_source, gt, ga_s, ga_r)
    for slot in range(2):
        spread_end(lambda target, slot=slot: mb.at[slot, target], rb.at[slot], pa_s.at[slot], pa_r.at[slot])

        @pl.when(me < UNITS)
        def _(slot=slot):
            for n in range(len(offsets)):
                remote(
                    xb.at[slot, peer(n)], xr.at[slot, me], xa_s.at[slot, n], xa_r.at[slot, me], rank_device(peer(n))
                ).wait_send()

    for copy in stores:
        copy.wait()


def solution(mesh):
    count = mesh.shape["blk"]
    nz, na = count // 4, mesh.shape["axial"]
    split = Mesh(mesh.devices.reshape(nz, 2, 2, na), (*BLK, "axial"))
    ranks = nz * 2

    def on_device(fields, inv_volume, radius_ratio, time_step, jac_circ, jac_other):
        layers = fields.shape[1]
        vmem = lambda *shape: pltpu.VMEM(shape, F32)
        dma = lambda *shape: pltpu.SemaphoreType.DMA(shape)
        plane = (layers, LANES)
        cell = (SUB, LANES)
        peers = ranks - 1
        scratch = [
            vmem(NV, ROWS + 4, *plane),
            vmem(NV, ROWS + 4, *plane),
            vmem(ROWS, *plane),
            vmem(ROWS + 2, *plane),
            vmem(ROWS + 4, *plane),
            vmem(ROWS, *plane),
            vmem(ROWS, *plane),
            vmem(ROWS, *plane),
            vmem(NV, ROWS, *plane),
            vmem(2, NV, *plane),
            vmem(2, NV, *plane),
            vmem(2, TILES, 2, *cell),
            vmem(2, 2, TILES, 2, *cell),
            vmem(2, TILES, NV, 2, *cell),
            vmem(2, HALF, NV, 2, *cell),
            vmem(2, UNITS, 2, *cell),
            vmem(2, ranks, 2, *cell),
            vmem(2, ranks, 2, *cell),
            vmem(2, UNITS, 2, *cell),
            vmem(2, TILES, NV, 2, *cell),
            vmem(TILES, 3, *cell),
            vmem(HALF, 3, *cell),
            vmem(2, HALF, 5, *cell),
            vmem(ranks, 3, *cell),
            vmem(2 * ranks, 4, *cell),
            vmem(2 * ranks, 2, *cell),
            vmem(2 * ranks, 2, *cell),
            vmem(2, HALF, NV, 2, *cell),
            dma(4, ROWS),
            dma(ROWS),
            dma(3, 2),
            dma(3, 2),
            dma(2, 2),
            dma(2, 2),
            dma(2),
            dma(2),
            pltpu.SemaphoreType.DMA,
            pltpu.SemaphoreType.DMA,
            dma(peers),
            dma(ranks),
            dma(2),
            dma(2),
            dma(2, peers),
            dma(2, ranks),
            dma(2, peers),
            dma(2, ranks),
            dma(2),
            dma(2),
        ]
        anywhere = pl.BlockSpec(memory_space=pl.ANY)
        scalars = pl.BlockSpec(memory_space=pltpu.SMEM)
        return pl.pallas_call(
            functools.partial(kernel, nz, na),
            out_shape=jax.ShapeDtypeStruct(fields.shape, F32),
            in_specs=[anywhere] * 4 + [scalars] * 2,
            out_specs=anywhere,
            scratch_shapes=scratch,
            compiler_params=pltpu.CompilerParams(collective_id=0, has_side_effects=True),
        )(fields, inv_volume, radius_ratio, time_step, jac_circ, jac_other)

    return jax.shard_map(
        on_device,
        mesh=split,
        in_specs=(
            P(None, None, BLK, "axial"),
            P(None, BLK, "axial"),
            P(None, BLK, "axial"),
            P(None, BLK, "axial"),
            P(),
            P(),
        ),
        out_specs=P(None, None, BLK, "axial"),
        check_vma=False,
    )
```

profile of v0, /device:TPU:1, one launch (start us, length us, event | category | flops | bytes accessed | tf_op | source)
XLA Modules:
  0.0 76.6 jit_solution(7510401235247913553)
XLA Ops:
  0.0 1.3 %copy.7.jac_o = f32[2,5,5]{2,1,0:T(8,128)} copy(f32[2,5,5]{2,0,1:T(2,128)} %param.11) | data formatting | bytes 400 | tf_op args[5]
  1.3 73.1 %shard_map.64 = f32[5,48,8,128]{3,2,1,0:T(8,128)} custom-call(f32[5,48,8,128]{3,2,1,0:T(8,128)} %fields.1, f32[48,8,128]{2,1,0:T(8,128)} %inv_volume.1, f32[48,8,128]{2,1,0:T(8,128)} %radius_ratio.1, f32[48,8,128]{2,1,0:T(8,128)} %time_step.1, f32[5,5]{1,0:T(8,128)} %jac_c.1, f32[2,5,5]{2,1,0:T(8,128)} %copy.7.jac_o), custom_call_target="tpu_custom_call" | custom-call | tf_op jit(solution)/shard_map/pallas_call | solution.py:592
  74.4 2.2 %copy.9 = f32[5,48,8,128]{3,2,1,0:T(8,128)} copy(f32[5,48,8,128]{3,2,1,0:T(8,128)} %shard_map.64) | data formatting | bytes 1966080
where the time goes:
time: 76.8 us; the launch traced here: 76.6 us
  Pallas kernels  73.1 us (95%)
  local copies, waits for them, and re-layouts  3.5 us (5%)
    pallas_call x1, Pallas kernels, on_device(): pl.pallas_call(functools.partial(kernel, nz, na), out_shape=jax.ShapeDtyp...  73.1 us
    unnamed x2, local copies, waits for them, and re-layouts  3.5 us

commit v1 on v0

--- a/solution.py
+++ b/solution.py
@@ -62,8 +62,12 @@
     tp,
     tx,
     res,
+    tab,
+    edge,
     in_sem,
     out_sem,
+    uc_s,
+    uc_r,
     circ_s,
     circ_r,
     ax_s,
@@ -153,28 +157,38 @@
         scaled = COURANT_RATIO * (1.0 + jnp.exp(SCALING_POWER * jnp.log(ratio)))
         return 1.0 / (0.25 * (scaled * scaled - 1.0))
 
-    def pack(u, t, slot):
-        for half in range(2):
-            packed = jnp.zeros((SUB, LANES), F32)
-            for n in range(NV * ROWS // 2):
-                flat = half * (NV * ROWS // 2) + n
-                moved = pltpu.roll(u[flat // ROWS, flat % ROWS + 2, tile(t)], 4 * n + 2, 1)
-                packed = jnp.where(lane // 4 == n, moved, packed)
-            pk[slot, t, half] = packed
+    def pack(u, t, carry):
+        packed = list(carry)
+        group = lane // 2 - t * ROWS
+        for v in range(NV):
+            for i in range(ROWS):
+                moved = pltpu.roll(u[v, i + 2, tile(t)], 2 * (t * ROWS + i) + 2, 1)
+                packed[v] = jnp.where(group == i, moved, packed[v])
+                packed[NV + v] = jnp.where(group == i + 1, moved, packed[NV + v])
+        return tuple(packed)
+
+    def keep_packed(slot, packed):
+        for v in range(NV):
+            pk[slot, 0, v] = packed[v]
+            pk[slot, 1, v] = packed[NV + v]
+
+    blank = (jnp.zeros((SUB, LANES), F32),) * (2 * NV)
+
+    for v in range(NV):
+        for m in range(NV):
+            tab[0, v, m] = jnp.broadcast_to(jac_c[v, m], (SUB, LANES))
+            tab[1, v, m] = jnp.broadcast_to(0.5 * jac_o[v, 0, m], (SUB, LANES))
+            tab[2, v, m] = jnp.broadcast_to(0.5 * jac_o[v, 1, m], (SUB, LANES))
 
     for copy in loads["u"]:
         copy.wait()
 
-    def pack_step(t, carry):
-        pack(u1, t, 0)
-        return carry
-
-    lax.fori_loop(0, TILES, pack_step, 0)
+    keep_packed(0, lax.fori_loop(0, TILES, functools.partial(pack, u1), blank))
     pl.semaphore_wait(barrier, len(greet))
 
-    def circ_pair(ref, which, low, high, width, axis):
+    def circ_pair(ref, which, low, width):
         def part(start):
-            return ref.at[:, pl.ds(start, width)] if axis == 1 else ref.at[pl.ds(start, width)]
+            return ref.at[pl.ds(start, width)]
 
         count = ROWS
         to_left = remote(part(low), part(low + count), circ_s.at[which, 0], circ_r.at[which, 0], left)
@@ -182,9 +196,17 @@
         return [to_left, to_right]
 
     def axial_pair(slot):
-        up = remote(pk.at[slot], pkh.at[slot, 0], ax_s.at[slot, 0], ax_r.at[slot, 0], ax_up)
-        down = remote(pk.at[slot], pkh.at[slot, 1], ax_s.at[slot, 1], ax_r.at[slot, 1], ax_down)
+        up = remote(pk.at[slot, 0], pkh.at[slot, 0], ax_s.at[slot, 0], ax_r.at[slot, 0], ax_up)
+        down = remote(pk.at[slot, 1], pkh.at[slot, 1], ax_s.at[slot, 1], ax_r.at[slot, 1], ax_down)
         return [up, down]
+
+    def chunk_pair(t):
+        def part(start):
+            return u1.at[:, pl.ds(start, 2), tile(t)]
+
+        to_left = remote(part(2), part(ROWS + 2), uc_s.at[0, t], uc_r.at[0, t], left)
+        to_right = remote(part(ROWS), part(0), uc_s.at[1, t], uc_r.at[1, t], right)
+        return [to_left, to_right]
 
     pending = []
 
@@ -194,10 +216,126 @@
         pending.extend(copies)
         return copies
 
-    u_halo = begin(circ_pair(u1, 0, 2, 2, 2, 1))
+    other = HALF * (1 - c)
+    mine = HALF * c
+
+    def chunk_send(step, carry):
+        for copy in chunk_pair((step + mine) % TILES):
+            copy.start()
+        return carry
+
     ax_halo = begin(axial_pair(0))
+    lax.fori_loop(0, TILES, chunk_send, 0)
     for copy in loads["rad"] + loads["vol"]:
         copy.wait()
+
+    def splat(value):
+        return jnp.broadcast_to(value, (SUB, LANES))
+
+    def local_step(u, slot, t, carry):
+        above = jnp.minimum(t * SUB + SUB, TILES * SUB - 1)
+        below = jnp.maximum(t * SUB - 1, 0)
+        for i in range(ROWS):
+            total = [None] * NV
+            for m in range(NV):
+
+                def row(k):
+                    return u[m, k + 2, tile(t)] if slot == 1 or 0 <= k < ROWS else None
+
+                def minus(p, q):
+                    if p is None:
+                        return -q
+                    return p if q is None else p - q
+
+                centre = u[m, i + 2, tile(t)]
+                circ = (2.0 / 3.0) * minus(row(i + 1), row(i - 1)) - (1.0 / 12.0) * minus(row(i + 2), row(i - 2))
+                plus1 = jnp.where(lane < LANES - 1, pltpu.roll(centre, LANES - 1, 1), 0.0)
+                plus2 = jnp.where(lane < LANES - 2, pltpu.roll(centre, LANES - 2, 1), 0.0)
+                minus1 = jnp.where(lane > 0, pltpu.roll(centre, 1, 1), 0.0)
+                minus2 = jnp.where(lane > 1, pltpu.roll(centre, 2, 1), 0.0)
+                axial = plus1 - minus1
+                fourth = (plus2 + minus2) - 4.0 * (plus1 + minus1) + 6.0 * centre
+                over = jnp.where(
+                    sub == SUB - 1, splat(u[m, i + 2, pl.ds(above, 1)]), pltpu.roll(centre, SUB - 1, 0)
+                )
+                under = jnp.where(sub == 0, splat(u[m, i + 2, pl.ds(below, 1)]), pltpu.roll(centre, 1, 0))
+                normal = over - under
+                for v in range(NV):
+                    term = tab[0, v, m] * circ + tab[1, v, m] * axial + tab[2, v, m] * normal
+                    if v == m:
+                        term = term + DISSIPATION * fourth
+                    total[v] = term if total[v] is None else total[v] + term
+            for v in range(NV):
+                yy[v, i, tile(t)] = total[v]
+        return carry
+
+    def mix(which, values):
+        out_values = []
+        for v in range(NV):
+            total = tab[which, v, 0] * values[0]
+            for m in range(1, NV):
+                total = total + tab[which, v, m] * values[m]
+            out_values.append(total)
+        return out_values
+
+    def edge_fluxes(slot):
+        even = lane % 2 == 0
+        low_edge = jnp.broadcast_to(a == 0, (SUB, LANES))
+        high_edge = jnp.broadcast_to(a == na - 1, (SUB, LANES))
+        low = [jnp.where(low_edge, 0.0, pkh[slot, 0, v]) for v in range(NV)]
+        high = [pltpu.roll(jnp.where(high_edge, 0.0, pkh[slot, 1, v]), LANES - 2, 1) for v in range(NV)]
+        low_next = [pltpu.roll(value, LANES - 1, 1) for value in low]
+        high_next = [pltpu.roll(value, 1, 1) for value in high]
+        low_flux = mix(1, [jnp.where(even, -value, 0.0) for value in low_next])
+        high_flux = mix(1, [jnp.where(even, 0.0, value) for value in high_next])
+        for v in range(NV):
+            low_total = low_flux[v] + DISSIPATION * jnp.where(even, low[v] - 4.0 * low_next[v], low[v])
+            high_total = high_flux[v] + DISSIPATION * jnp.where(even, high[v], high[v] - 4.0 * high_next[v])
+            for half in range(2):
+                index = (lane // 4) * 2 + lane % 2 + half * (HALF * ROWS * 2)
+                index = jnp.minimum(index, LANES - 1)
+                picked_low = jnp.take_along_axis(low_total, index, axis=1)
+                picked_high = jnp.take_along_axis(high_total, index, axis=1)
+                edge[half, v] = jnp.where(lane % 4 < 2, picked_high, picked_low)
+
+    def sweep_step(slot, t):
+        if slot == 0:
+            for copy in chunk_pair(t):
+                copy.wait_recv()
+            low2, low1, high1, high2 = ([u1[m, k, tile(t)] for m in range(NV)] for k in (0, 1, ROWS + 2, ROWS + 3))
+            twelfth = 1.0 / 12.0
+            extra = {
+                0: mix(0, [twelfth * p - (8.0 * twelfth) * q for p, q in zip(low2, low1)]),
+                1: mix(0, [twelfth * q for q in low1]),
+                ROWS - 2: mix(0, [-twelfth * q for q in high1]),
+                ROWS - 1: mix(0, [(8.0 * twelfth) * q - twelfth * p for p, q in zip(high2, high1)]),
+            }
+        near = (lane < 2) | (lane >= LANES - 2)
+        half = t // HALF
+        base = (t % HALF) * ROWS
+        ahead = [jnp.zeros((SUB, LANES), F32)] * NV
+        start = [jnp.zeros((SUB, LANES), F32)] * NV
+        product = jnp.ones((SUB, LANES), F32)
+        for i in range(ROWS):
+            weight = wgt[i, tile(t)]
+            ratio = cc[i, tile(t)]
+            for v in range(NV):
+                flux = yy[v, i, tile(t)]
+                if slot == 0 and i in extra:
+                    flux = flux + extra[i][v]
+                side = pltpu.roll(edge[half, v], LANES - 2 - 4 * (base + i), 1)
+                scaled = weight * (flux + jnp.where(near, side, 0.0))
+                if slot == 0 and i == 0:
+                    qrow[0, v, tile(t)] = scaled
+                if slot == 0 and i == ROWS - 1:
+                    qrow[1, v, tile(t)] = scaled
+                ahead[v] = (scaled + ahead[v]) * ratio
+                yy[v, i, tile(t)] = ahead[v]
+                start[v] = start[v] + product * ahead[v]
+            product = cp[i, tile(t)]
+        for v in range(NV):
+            pb[slot, t, v, 0] = start[v]
+            pb[slot, t, v, 1] = ahead[v]
 
     def factor_step(t, carry):
         ratio = jnp.zeros((SUB, LANES), F32)
@@ -218,13 +356,8 @@
         return carry
 
     lax.fori_loop(0, TILES, factor_step, 0)
-    other = 3 * (1 - c)
-    mine = 3 * c
     g_pair = begin([remote(gg.at[pl.ds(other, HALF)], gr, gp_s, gp_r, partner)])
-    for copy in loads["dt"]:
-        copy.wait()
-    rad_halo = begin(circ_pair(rad, 1, 1, 1, 1, 0))
-    dt_halo = begin(circ_pair(dt, 2, 2, 2, 2, 0))
+    lax.fori_loop(0, TILES, functools.partial(local_step, u1, 0), 0)
 
     def by_core(own, theirs):
         return jnp.where(core0, own, theirs), jnp.where(core0, theirs, own)
@@ -255,21 +388,22 @@
 
     lax.fori_loop(0, HALF, merge_step, 0)
 
-    def spread(src_of, dst, ssem, rsem):
-        for n in range(len(offsets)):
-            target = peer(n)
-
-            @pl.when(target < UNITS)
-            def _(n=n, target=target):
-                remote(src_of(target), dst.at[me], ssem.at[n], rsem.at[me], rank_device(target)).start()
+    def unit_send(src_of, dst, ssem, rsem, target):
+        return remote(src_of(target), dst.at[me], ssem.at[target], rsem.at[me], rank_device(target))
+
+    def spread(src_of, dst, ssem, rsem, targets):
+        for target in targets:
+
+            @pl.when(target != me)
+            def _(target=target):
+                unit_send(src_of, dst, ssem, rsem, target).start()
 
     def spread_end(src_of, dst, ssem, rsem):
-        for n in range(len(offsets)):
-            target = peer(n)
-
-            @pl.when(target < UNITS)
-            def _(n=n, target=target):
-                remote(src_of(target), dst.at[me], ssem.at[n], rsem.at[me], rank_device(target)).wait_send()
+        for target in range(UNITS):
+
+            @pl.when(target != me)
+            def _(target=target):
+                unit_send(src_of, dst, ssem, rsem, target).wait_send()
 
     def spread_recv(dst, rsem):
         for n in range(len(offsets)):
@@ -279,68 +413,11 @@
     def g_source(target):
         return gm.at[0, target // NV, pl.ds(0, 3)]
 
-    spread(g_source, gt, ga_s, ga_r)
-    for copy in u_halo + ax_halo:
-        copy.wait_recv()
-
-    def splat(value):
-        return jnp.broadcast_to(value, (SUB, LANES))
-
-    def residual_step(u, slot, t, carry):
-        edges = []
-        low_edge = jnp.broadcast_to(a == 0, (SUB, LANES))
-        high_edge = jnp.broadcast_to(a == na - 1, (SUB, LANES))
-        for half in range(2):
-            from_low = jnp.where(low_edge, 0.0, pkh[slot, 0, t, half])
-            from_high = jnp.where(high_edge, 0.0, pkh[slot, 1, t, half])
-            edges.append(jnp.where(lane % 4 < 2, from_low, from_high))
-        above = jnp.minimum(t * SUB + SUB, TILES * SUB - 1)
-        below = jnp.maximum(t * SUB - 1, 0)
-        ahead = [jnp.zeros((SUB, LANES), F32)] * NV
-        start = [jnp.zeros((SUB, LANES), F32)] * NV
-        product = jnp.ones((SUB, LANES), F32)
-        for i in range(ROWS):
-            total = [None] * NV
-            for m in range(NV):
-                centre = u[m, i + 2, tile(t)]
-                circ = (2.0 / 3.0) * (u[m, i + 3, tile(t)] - u[m, i + 1, tile(t)]) - (1.0 / 12.0) * (
-                    u[m, i + 4, tile(t)] - u[m, i, tile(t)]
-                )
-                flat = m * ROWS + i
-                half, n = flat // (NV * ROWS // 2), flat % (NV * ROWS // 2)
-                edge = pltpu.roll(edges[half], LANES - (4 * n + 2), 1)
-                plus1 = pltpu.roll(jnp.where(lane < 1, edge, centre), LANES - 1, 1)
-                plus2 = pltpu.roll(jnp.where(lane < 2, edge, centre), LANES - 2, 1)
-                minus1 = pltpu.roll(jnp.where(lane > LANES - 2, edge, centre), 1, 1)
-                minus2 = pltpu.roll(jnp.where(lane > LANES - 3, edge, centre), 2, 1)
-                axial = plus1 - minus1
-                fourth = (plus2 + minus2) - 4.0 * (plus1 + minus1) + 6.0 * centre
-                over = jnp.where(
-                    sub == SUB - 1, splat(u[m, i + 2, pl.ds(above, 1)]), pltpu.roll(centre, SUB - 1, 0)
-                )
-                under = jnp.where(sub == 0, splat(u[m, i + 2, pl.ds(below, 1)]), pltpu.roll(centre, 1, 0))
-                normal = over - under
-                for v in range(NV):
-                    term = jac_c[v, m] * circ + (0.5 * jac_o[0, v, m]) * axial + (0.5 * jac_o[1, v, m]) * normal
-                    if v == m:
-                        term = term + DISSIPATION * fourth
-                    total[v] = term if total[v] is None else total[v] + term
-            weight = wgt[i, tile(t)]
-            ratio = cc[i, tile(t)]
-            for v in range(NV):
-                scaled = weight * total[v]
-                if slot == 0 and i == 0:
-                    qrow[0, v, tile(t)] = scaled
-                if slot == 0 and i == ROWS - 1:
-                    qrow[1, v, tile(t)] = scaled
-                ahead[v] = (scaled + ahead[v]) * ratio
-                yy[v, i, tile(t)] = ahead[v]
-                start[v] = start[v] + product * ahead[v]
-            product = cp[i, tile(t)]
-        for v in range(NV):
-            pb[slot, t, v, 0] = start[v]
-            pb[slot, t, v, 1] = ahead[v]
-        return carry
+    spread(g_source, gt, ga_s, ga_r, range(UNITS))
+    for copy in loads["dt"]:
+        copy.wait()
+    rad_halo = begin(circ_pair(rad, 0, 1, 1))
+    dt_halo = begin(circ_pair(dt, 1, 2, 2))
 
     def tree_factors():
         for r in range(ranks):
@@ -392,23 +469,51 @@
             for n in range(2):
                 xb[slot, r, n] = tx[r, n]
 
-    def section(slot, u):
-        lax.fori_loop(0, TILES, functools.partial(residual_step, u, slot), 0)
-        pair = begin([remote(pb.at[slot, pl.ds(other, HALF)], pr.at[slot], pp_s.at[slot], pp_r.at[slot], partner)])
-        pair[0].wait_recv()
-
-        def merge(t, carry):
-            a_cross, a_last, b_first, b_cross, d = (gm[1, t, n] for n in range(5))
+    def pair_copy(slot, step):
+        return remote(
+            pb.at[slot, other + step], pr.at[slot, step], pp_s.at[slot, step], pp_r.at[slot, step], partner
+        )
+
+    def back_copy(slot, step):
+        return remote(
+            res.at[slot, step], xx.at[slot, mine + step], xp_s.at[slot, step], xp_r.at[slot, step], partner
+        )
+
+    def arrival(slot, step):
+        return remote(
+            res.at[slot, step], xx.at[slot, other + step], xp_s.at[slot, step], xp_r.at[slot, step], partner
+        )
+
+    def section(slot):
+        edge_fluxes(slot)
+
+        def theirs(step, carry):
+            sweep_step(slot, other + step)
+            pair_copy(slot, step).start()
+            return carry
+
+        lax.fori_loop(0, HALF, theirs, 0)
+
+        def ours(step, carry):
+            sweep_step(slot, mine + step)
+            pair_copy(slot, step).wait_recv()
+            a_cross, a_last, b_first, b_cross, d = (gm[1, step, n] for n in range(5))
             for v in range(NV):
-                a_head, b_head = by_core(pb[slot, mine + t, v, 0], pr[slot, t, v, 0])
-                a_tail, b_tail = by_core(pb[slot, mine + t, v, 1], pr[slot, t, v, 1])
+                a_head, b_head = by_core(pb[slot, mine + step, v, 0], pr[slot, step, v, 0])
+                a_tail, b_tail = by_core(pb[slot, mine + step, v, 1], pr[slot, step, v, 1])
                 a0, b0 = inner_pair(a_tail, b_head, a_last, b_first, d)
-                mb[slot, t * NV + v, 0] = a_head + a_cross * b0
-                mb[slot, t * NV + v, 1] = b_tail + b_cross * a0
+                mb[slot, step * NV + v, 0] = a_head + a_cross * b0
+                mb[slot, step * NV + v, 1] = b_tail + b_cross * a0
+            spread(
+                lambda target: mb.at[slot, target],
+                rb.at[slot],
+                pa_s.at[slot],
+                pa_r.at[slot],
+                [step * NV + v for v in range(NV)],
+            )
             return carry
 
-        lax.fori_loop(0, HALF, merge, 0)
-        spread(lambda target: mb.at[slot, target], rb.at[slot], pa_s.at[slot], pa_r.at[slot])
+        lax.fori_loop(0, HALF, ours, 0)
 
         q_halo = []
         if slot == 0:
@@ -434,36 +539,35 @@
                     xb.at[slot, peer(n)], xr.at[slot, me], xa_s.at[slot, n], xa_r.at[slot, me], rank_device(peer(n))
                 ).start()
 
-        for n in range(len(offsets)):
-            origin = source(n)
-
-            @pl.when(origin < UNITS)
-            def _(origin=origin):
-                remote(
-                    xr.at[slot, origin], xr.at[slot, origin], xa_r.at[slot, origin], xa_r.at[slot, origin], rank_device(origin)
-                ).wait_recv()
-
-        def unmerge(t, carry):
-            a_cross, a_last, b_first, b_cross, d = (gm[1, t, n] for n in range(5))
+        def unmerge(step, carry):
             for v in range(NV):
-                xl, xh = xr[slot, t * NV + v, 0], xr[slot, t * NV + v, 1]
-                _, b_head = by_core(pb[slot, mine + t, v, 0], pr[slot, t, v, 0])
-                a_tail, _ = by_core(pb[slot, mine + t, v, 1], pr[slot, t, v, 1])
+                origin = step * NV + v
+
+                @pl.when(origin != me)
+                def _(origin=origin):
+                    remote(
+                        xr.at[slot, origin],
+                        xr.at[slot, origin],
+                        xa_r.at[slot, origin],
+                        xa_r.at[slot, origin],
+                        rank_device(origin),
+                    ).wait_recv()
+
+            a_cross, a_last, b_first, b_cross, d = (gm[1, step, n] for n in range(5))
+            for v in range(NV):
+                xl, xh = xr[slot, step * NV + v, 0], xr[slot, step * NV + v, 1]
+                _, b_head = by_core(pb[slot, mine + step, v, 0], pr[slot, step, v, 0])
+                a_tail, _ = by_core(pb[slot, mine + step, v, 1], pr[slot, step, v, 1])
                 mid_a, mid_b = inner_pair(a_tail + a_cross * xl, b_head + b_cross * xh, a_last, b_first, d)
-                xx[slot, mine + t, v, 0] = jnp.where(core0, xl, mid_a)
-                xx[slot, mine + t, v, 1] = jnp.where(core0, mid_b, xh)
-                res[slot, t, v, 0] = jnp.where(core0, mid_a, xl)
-                res[slot, t, v, 1] = jnp.where(core0, xh, mid_b)
+                xx[slot, mine + step, v, 0] = jnp.where(core0, xl, mid_a)
+                xx[slot, mine + step, v, 1] = jnp.where(core0, mid_b, xh)
+                res[slot, step, v, 0] = jnp.where(core0, mid_a, xl)
+                res[slot, step, v, 1] = jnp.where(core0, xh, mid_b)
+            back_copy(slot, step).start()
             return carry
 
         lax.fori_loop(0, HALF, unmerge, 0)
-        back = begin(
-            [remote(res.at[slot], xx.at[slot, pl.ds(mine, HALF)], xp_s.at[slot], xp_r.at[slot], partner)]
-        )
-        arrival = remote(res.at[slot], xx.at[slot, pl.ds(other, HALF)], xp_s.at[slot], xp_r.at[slot], partner)
-        arrival.wait_recv()
-        for copy in q_halo:
-            copy.wait_recv()
+        return q_halo
 
     def sweep(slot, t, v):
         low, high = xx[slot, t, v, 0], xx[slot, t, v, 1]
@@ -474,8 +578,10 @@
             values[i] = later
         return low, high, values
 
-    section(0, u1)
-    for copy in rad_halo + dt_halo:
+    for copy in ax_halo:
+        copy.wait_recv()
+    q_halo = section(0)
+    for copy in q_halo + rad_halo + dt_halo:
         copy.wait_recv()
 
     def update_one(t, carry):
@@ -487,31 +593,58 @@
             high2 = diag_high * high - values[ROWS - 1] - qhalo[1, v, tile(t)]
             for i, value in enumerate([low2, low] + values + [high, high2]):
                 u2[v, i, tile(t)] = u1[v, i, tile(t)] + SECTION_ONE * dt[i, tile(t)] * value
-        pack(u2, t, 1)
-        return carry
-
-    lax.fori_loop(0, TILES, update_one, 0)
+        return pack(u2, t, carry)
+
+    def update_one_late(step, carry):
+        arrival(0, step).wait_recv()
+        return update_one(other + step, carry)
+
+    packed = lax.fori_loop(0, HALF, lambda step, carry: update_one(mine + step, carry), blank)
+    packed = lax.fori_loop(0, HALF, update_one_late, packed)
+    keep_packed(1, packed)
     ax_halo = begin(axial_pair(1))
+    lax.fori_loop(0, TILES, functools.partial(local_step, u2, 1), 0)
     for copy in ax_halo:
         copy.wait_recv()
-    section(1, u2)
+    section(1)
+
+    def stores(t):
+        return [
+            pltpu.make_async_copy(u2.at[:, i + 2, tile(t)], out.at[:, tile(t), i, :], out_sem.at[t, i])
+            for i in range(ROWS)
+        ]
 
     def update_two(t, carry):
         for v in range(NV):
             _, _, values = sweep(1, t, v)
             for i, value in enumerate(values):
                 u2[v, i + 2, tile(t)] = u1[v, i + 2, tile(t)] + dt[i + 2, tile(t)] * value
+        for copy in stores(t):
+            copy.start()
         return carry
 
-    lax.fori_loop(0, TILES, update_two, 0)
-    stores = [pltpu.make_async_copy(u2.at[:, i + 2], out.at[:, :, i, :], out_sem.at[i]) for i in range(ROWS)]
-    for copy in stores:
-        copy.start()
+    def update_two_late(step, carry):
+        arrival(1, step).wait_recv()
+        return update_two(other + step, carry)
+
+    lax.fori_loop(0, HALF, lambda step, carry: update_two(mine + step, carry), 0)
+    lax.fori_loop(0, HALF, update_two_late, 0)
+
     for copy in pending:
         copy.wait_send()
     spread_end(g_source, gt, ga_s, ga_r)
+
+    def sent(t, carry):
+        for copy in chunk_pair(t):
+            copy.wait_send()
+        return carry
+
+    lax.fori_loop(0, TILES, sent, 0)
     for slot in range(2):
         spread_end(lambda target, slot=slot: mb.at[slot, target], rb.at[slot], pa_s.at[slot], pa_r.at[slot])
+        for step in range(HALF):
+            pair_copy(slot, step).wait_send()
+            back_copy(slot, step).wait_send()
 
         @pl.when(me < UNITS)
         def _(slot=slot):
@@ -520,8 +653,12 @@
                     xb.at[slot, peer(n)], xr.at[slot, me], xa_s.at[slot, n], xa_r.at[slot, me], rank_device(peer(n))
                 ).wait_send()
 
-    for copy in stores:
-        copy.wait()
+    def stored(t, carry):
+        for copy in stores(t):
+            copy.wait()
+        return carry
+
+    lax.fori_loop(0, TILES, stored, 0)
 
 
 def solution(mesh):
@@ -549,8 +686,8 @@
             vmem(NV, ROWS, *plane),
             vmem(2, NV, *plane),
             vmem(2, NV, *plane),
-            vmem(2, TILES, 2, *cell),
-            vmem(2, 2, TILES, 2, *cell),
+            vmem(2, 2, NV, *cell),
+            vmem(2, 2, NV, *cell),
             vmem(2, TILES, NV, 2, *cell),
             vmem(2, HALF, NV, 2, *cell),
             vmem(2, UNITS, 2, *cell),
@@ -566,26 +703,30 @@
             vmem(2 * ranks, 2, *cell),
             vmem(2 * ranks, 2, *cell),
             vmem(2, HALF, NV, 2, *cell),
+            vmem(3, NV, NV, *cell),
+            vmem(2, NV, *cell),
             dma(4, ROWS),
-            dma(ROWS),
-            dma(3, 2),
-            dma(3, 2),
+            dma(TILES, ROWS),
+            dma(2, TILES),
+            dma(2, TILES),
+            dma(2, 2),
+            dma(2, 2),
             dma(2, 2),
             dma(2, 2),
             dma(2),
             dma(2),
             pltpu.SemaphoreType.DMA,
             pltpu.SemaphoreType.DMA,
-            dma(peers),
+            dma(UNITS),
             dma(ranks),
-            dma(2),
-            dma(2),
-            dma(2, peers),
+            dma(2, HALF),
+            dma(2, HALF),
+            dma(2, UNITS),
             dma(2, ranks),
             dma(2, peers),
             dma(2, ranks),
-            dma(2),
-            dma(2),
+            dma(2, HALF),
+            dma(2, HALF),
         ]
         anywhere = pl.BlockSpec(memory_space=pl.ANY)
         scalars = pl.BlockSpec(memory_space=pltpu.SMEM)
@@ -596,7 +737,7 @@
             out_specs=anywhere,
             scratch_shapes=scratch,
             compiler_params=pltpu.CompilerParams(collective_id=0, has_side_effects=True),
-        )(fields, inv_volume, radius_ratio, time_step, jac_circ, jac_other)
+        )(fields, inv_volume, radius_ratio, time_step, jac_circ, jnp.transpose(jac_other, (1, 0, 2)))
 
     return jax.shard_map(
         on_device,

time: 76.8 us -> 60.5 us (0.79)
  Pallas kernels: 73.1 us -> 58.1 us
  local copies, waits for them, and re-layouts: 3.5 us -> 2.21 us
    pallas_call x1, Pallas kernels: 73.1 us -> 58.1 us  [on_device(): pl.pallas_call(functools.partial(kernel, nz, na), out_shape=jax.ShapeDtyp...]
    unnamed x2 -> x1, local copies, waits for them, and re-layouts: 3.5 us -> 2.21 us
where the time goes in v1:
time: 60.5 us; the launch traced here: 60.4 us
  Pallas kernels  58.1 us (96%)
  local copies, waits for them, and re-layouts  2.21 us (4%)
    pallas_call x1, Pallas kernels, on_device(): pl.pallas_call(functools.partial(kernel, nz, na), out_shape=jax.ShapeDtyp...  58.1 us
    unnamed x1, local copies, waits for them, and re-layouts  2.21 us

profile of v1, /device:TPU:1, one launch (start us, length us, event | category | flops | bytes accessed | tf_op | source)
XLA Modules:
  0.0 60.4 jit_solution(14769551604682556469)
XLA Ops:
  0.0 58.1 %shard_map.64 = f32[5,48,8,128]{3,2,1,0:T(8,128)} custom-call(f32[5,48,8,128]{3,2,1,0:T(8,128)} %fields.1, f32[48,8,128]{2,1,0:T(8,128)} %inv_volume.1, f32[48,8,128]{2,1,0:T(8,128)} %radius_ratio.1, f32[48,8,128]{2,1,0:T(8,128)} %time_step.1, f32[5,5]{1,0:T(8,128)} %jac_c.1, f32[5,2,5]{2,1,0:T(2,128)} %bitcast.1), custom_call_target="tpu_custom_call" | custom-call | tf_op jit(solution)/shard_map/pallas_call | solution.py:733
  58.2 2.2 %copy.8 = f32[5,48,8,128]{3,2,1,0:T(8,128)} copy(f32[5,48,8,128]{3,2,1,0:T(8,128)} %shard_map.64) | data formatting | bytes 1966080

commit v2 on v1

--- a/solution.py
+++ b/solution.py
@@ -19,6 +19,7 @@
 HALF = 3
 ROWS = 8
 SUB = 8
+SPLIT = 2
 LANES = 128
 UNITS = HALF * NV
 F32 = jnp.float32
@@ -86,6 +87,7 @@
     xa_r,
     xp_s,
     xp_r,
+    ready,
 ):
     ranks = nz * 2
     z = lax.axis_index("blk_0")
@@ -131,20 +133,38 @@
             device_id_type=pl.DeviceIdType.MESH,
         )
 
-    loads = {
-        "rad": [pltpu.make_async_copy(radius_ratio.at[:, i, :], rad.at[i + 1], in_sem.at[0, i]) for i in range(ROWS)],
-        "vol": [pltpu.make_async_copy(inv_volume.at[:, i, :], vol.at[i], in_sem.at[1, i]) for i in range(ROWS)],
-        "u": [pltpu.make_async_copy(fields.at[:, :, i, :], u1.at[:, i + 2], in_sem.at[2, i]) for i in range(ROWS)],
-        "dt": [pltpu.make_async_copy(time_step.at[:, i, :], dt.at[i + 2], in_sem.at[3, i]) for i in range(ROWS)],
-    }
-    for name in ("u", "rad", "vol", "dt"):
-        for copy in loads[name]:
-            copy.start()
+    def load_u(i, group):
+        pltpu.make_async_copy(fields.at[:, :, i, :], u1.at[:, i + 2], in_sem.at[group]).start()
+
+    def load_cell(source_ref, target_ref, shift, group):
+        for i in range(ROWS):
+            pltpu.make_async_copy(source_ref.at[:, i, :], target_ref.at[i + shift], in_sem.at[group]).start()
+
+    def landed(part, semaphore):
+        pltpu.make_async_copy(part, part, semaphore).wait()
+
+    def beside(dz, dy):
+        return rank_device(((z + nz + dz) % nz) * 2 + (y + dy) % 2)
+
+    def signal(semaphore, device):
+        pl.semaphore_signal(semaphore, inc=1, device_id=device, device_id_type=pl.DeviceIdType.MESH)
 
     barrier = pltpu.get_barrier_semaphore()
-    greet = [left, right, ax_up, ax_down, partner] + [rank_device(peer(n)) for n in range(len(offsets))]
+    greet = [ax_up, ax_down, right, left, beside(1, 1), beside(-1, 1), beside(1, 0), beside(-1, 0), beside(0, 1), partner]
+    edge_rows, inner_rows = (0, 1, ROWS - 2, ROWS - 1), range(2, ROWS - 2)
+    for i in edge_rows:
+        load_u(i, 0)
     for device in greet:
-        pl.semaphore_signal(barrier, inc=1, device_id=device, device_id_type=pl.DeviceIdType.MESH)
+        signal(barrier, device)
+    for i in inner_rows:
+        load_u(i, 1)
+
+    def ready_signal(n):
+        for dz in (1, -1):
+            signal(ready.at[n], beside(dz, 0))
+
+    def ready_wait(n):
+        pl.semaphore_wait(ready.at[n], 2)
 
     lane = lax.broadcasted_iota(jnp.int32, (SUB, LANES), 1)
     sub = lax.broadcasted_iota(jnp.int32, (SUB, LANES), 0)
@@ -174,16 +194,7 @@
 
     blank = (jnp.zeros((SUB, LANES), F32),) * (2 * NV)
 
-    for v in range(NV):
-        for m in range(NV):
-            tab[0, v, m] = jnp.broadcast_to(jac_c[v, m], (SUB, LANES))
-            tab[1, v, m] = jnp.broadcast_to(0.5 * jac_o[v, 0, m], (SUB, LANES))
-            tab[2, v, m] = jnp.broadcast_to(0.5 * jac_o[v, 1, m], (SUB, LANES))
-
-    for copy in loads["u"]:
-        copy.wait()
-
-    keep_packed(0, lax.fori_loop(0, TILES, functools.partial(pack, u1), blank))
+    landed(u1.at[:, pl.ds(2, len(edge_rows))], in_sem.at[0])
     pl.semaphore_wait(barrier, len(greet))
 
     def circ_pair(ref, which, low, width):
@@ -224,10 +235,22 @@
             copy.start()
         return carry
 
+    lax.fori_loop(0, TILES, chunk_send, 0)
+    ready_signal(0)
+    load_cell(radius_ratio, rad, 1, 2)
+    load_cell(inv_volume, vol, 0, 3)
+    landed(u1.at[:, pl.ds(2, len(inner_rows))], in_sem.at[1])
+    keep_packed(0, lax.fori_loop(0, TILES, functools.partial(pack, u1), blank))
     ax_halo = begin(axial_pair(0))
-    lax.fori_loop(0, TILES, chunk_send, 0)
-    for copy in loads["rad"] + loads["vol"]:
-        copy.wait()
+    for v in range(NV):
+        for m in range(NV):
+            tab[0, v, m] = jnp.broadcast_to(jac_c[v, m] / 12.0, (SUB, LANES))
+            tab[1, v, m] = jnp.broadcast_to(0.5 * jac_o[v, 0, m], (SUB, LANES))
+            tab[2, v, m] = jnp.broadcast_to(0.5 * jac_o[v, 1, m], (SUB, LANES))
+
+    load_cell(time_step, dt, 2, 4)
+    landed(rad.at[pl.ds(1, ROWS)], in_sem.at[2])
+    landed(vol, in_sem.at[3])
 
     def splat(value):
         return jnp.broadcast_to(value, (SUB, LANES))
@@ -248,11 +271,11 @@
                     return p if q is None else p - q
 
                 centre = u[m, i + 2, tile(t)]
-                circ = (2.0 / 3.0) * minus(row(i + 1), row(i - 1)) - (1.0 / 12.0) * minus(row(i + 2), row(i - 2))
-                plus1 = jnp.where(lane < LANES - 1, pltpu.roll(centre, LANES - 1, 1), 0.0)
-                plus2 = jnp.where(lane < LANES - 2, pltpu.roll(centre, LANES - 2, 1), 0.0)
-                minus1 = jnp.where(lane > 0, pltpu.roll(centre, 1, 1), 0.0)
-                minus2 = jnp.where(lane > 1, pltpu.roll(centre, 2, 1), 0.0)
+                circ = 8.0 * minus(row(i + 1), row(i - 1)) - minus(row(i + 2), row(i - 2))
+                plus1 = pltpu.roll(centre, LANES - 1, 1)
+                plus2 = pltpu.roll(centre, LANES - 2, 1)
+                minus1 = pltpu.roll(centre, 1, 1)
+                minus2 = pltpu.roll(centre, 2, 1)
                 axial = plus1 - minus1
                 fourth = (plus2 + minus2) - 4.0 * (plus1 + minus1) + 6.0 * centre
                 over = jnp.where(
@@ -282,8 +305,10 @@
         even = lane % 2 == 0
         low_edge = jnp.broadcast_to(a == 0, (SUB, LANES))
         high_edge = jnp.broadcast_to(a == na - 1, (SUB, LANES))
-        low = [jnp.where(low_edge, 0.0, pkh[slot, 0, v]) for v in range(NV)]
-        high = [pltpu.roll(jnp.where(high_edge, 0.0, pkh[slot, 1, v]), LANES - 2, 1) for v in range(NV)]
+        low = [jnp.where(low_edge, 0.0, pkh[slot, 0, v]) - pk[slot, 0, v] for v in range(NV)]
+        high = [
+            pltpu.roll(jnp.where(high_edge, 0.0, pkh[slot, 1, v]) - pk[slot, 1, v], LANES - 2, 1) for v in range(NV)
+        ]
         low_next = [pltpu.roll(value, LANES - 1, 1) for value in low]
         high_next = [pltpu.roll(value, 1, 1) for value in high]
         low_flux = mix(1, [jnp.where(even, -value, 0.0) for value in low_next])
@@ -303,12 +328,11 @@
             for copy in chunk_pair(t):
                 copy.wait_recv()
             low2, low1, high1, high2 = ([u1[m, k, tile(t)] for m in range(NV)] for k in (0, 1, ROWS + 2, ROWS + 3))
-            twelfth = 1.0 / 12.0
             extra = {
-                0: mix(0, [twelfth * p - (8.0 * twelfth) * q for p, q in zip(low2, low1)]),
-                1: mix(0, [twelfth * q for q in low1]),
-                ROWS - 2: mix(0, [-twelfth * q for q in high1]),
-                ROWS - 1: mix(0, [(8.0 * twelfth) * q - twelfth * p for p, q in zip(high2, high1)]),
+                0: mix(0, [p - 8.0 * q for p, q in zip(low2, low1)]),
+                1: mix(0, low1),
+                ROWS - 2: mix(0, [-q for q in high1]),
+                ROWS - 1: mix(0, [8.0 * q - p for p, q in zip(high2, high1)]),
             }
         near = (lane < 2) | (lane >= LANES - 2)
         half = t // HALF
@@ -357,7 +381,11 @@
 
     lax.fori_loop(0, TILES, factor_step, 0)
     g_pair = begin([remote(gg.at[pl.ds(other, HALF)], gr, gp_s, gp_r, partner)])
-    lax.fori_loop(0, TILES, functools.partial(local_step, u1, 0), 0)
+    ready_wait(0)
+    ready_signal(1)
+    lax.fori_loop(0, SPLIT, functools.partial(local_step, u1, 0), 0)
+    ready_wait(1)
+    ready_signal(2)
 
     def by_core(own, theirs):
         return jnp.where(core0, own, theirs), jnp.where(core0, theirs, own)
@@ -388,36 +416,37 @@
 
     lax.fori_loop(0, HALF, merge_step, 0)
 
-    def unit_send(src_of, dst, ssem, rsem, target):
-        return remote(src_of(target), dst.at[me], ssem.at[target], rsem.at[me], rank_device(target))
-
     def spread(src_of, dst, ssem, rsem, targets):
         for target in targets:
 
             @pl.when(target != me)
             def _(target=target):
-                unit_send(src_of, dst, ssem, rsem, target).start()
-
-    def spread_end(src_of, dst, ssem, rsem):
-        for target in range(UNITS):
-
-            @pl.when(target != me)
-            def _(target=target):
-                unit_send(src_of, dst, ssem, rsem, target).wait_send()
-
-    def spread_recv(dst, rsem):
-        for n in range(len(offsets)):
-            origin = source(n)
-            remote(dst.at[origin], dst.at[origin], rsem.at[origin], rsem.at[origin], rank_device(origin)).wait_recv()
+                remote(src_of(target), dst.at[me], ssem, rsem, rank_device(target)).start()
+
+    def group_recv(dst, rsem, count):
+        part = dst.at[pl.ds(0, count)]
+        remote(part, part, rsem, rsem, partner).wait_recv()
+
+    def group_sent(src, ssem, count):
+        part = src.at[pl.ds(0, count)]
+        remote(part, part, ssem, ssem, partner).wait_send()
+
+    def spread_end(src, ssem):
+        @pl.when(me < UNITS)
+        def _():
+            group_sent(src, ssem, UNITS - 1)
+
+        @pl.when(me >= UNITS)
+        def _():
+            group_sent(src, ssem, UNITS)
 
     def g_source(target):
         return gm.at[0, target // NV, pl.ds(0, 3)]
 
+    ready_wait(2)
     spread(g_source, gt, ga_s, ga_r, range(UNITS))
-    for copy in loads["dt"]:
-        copy.wait()
-    rad_halo = begin(circ_pair(rad, 0, 1, 1))
-    dt_halo = begin(circ_pair(dt, 1, 2, 2))
+    lax.fori_loop(SPLIT, TILES, functools.partial(local_step, u1, 0), 0)
+    landed(dt.at[pl.ds(2, ROWS)], in_sem.at[4])
 
     def tree_factors():
         for r in range(ranks):
@@ -484,6 +513,31 @@
             res.at[slot, step], xx.at[slot, other + step], xp_s.at[slot, step], xp_r.at[slot, step], partner
         )
 
+    def section_sent(slot):
+        spread_end(mb.at[slot], pa_s.at[slot])
+
+        @pl.when(me < UNITS)
+        def _():
+            group_sent(xb.at[slot], xa_s.at[slot], ranks - 1)
+
+        for step in range(HALF):
+            pair_copy(slot, step).wait_send()
+            back_copy(slot, step).wait_send()
+
+    def first_sent():
+        for copy in pending:
+            copy.wait_send()
+        pending.clear()
+        spread_end(gt, ga_s)
+
+        def sent(t, carry):
+            for copy in chunk_pair(t):
+                copy.wait_send()
+            return carry
+
+        lax.fori_loop(0, TILES, sent, 0)
+        section_sent(0)
+
     def section(slot):
         edge_fluxes(slot)
 
@@ -518,40 +572,40 @@
         q_halo = []
         if slot == 0:
             q_halo = begin(
-                [
+                circ_pair(rad, 0, 1, 1)
+                + circ_pair(dt, 1, 2, 2)
+                + [
                     remote(qrow.at[0], qhalo.at[1], q_s.at[0], q_r.at[0], left),
                     remote(qrow.at[1], qhalo.at[0], q_s.at[1], q_r.at[1], right),
                 ]
             )
 
+        if slot == 1:
+            first_sent()
+
         @pl.when(me < UNITS)
         def _():
             if slot == 0:
                 gt[me] = gm[0, me // NV, pl.ds(0, 3)]
-                spread_recv(gt, ga_r)
+                group_recv(gt, ga_r, ranks - 1)
                 tree_factors()
             rb[slot, me] = mb[slot, me]
-            spread_recv(rb.at[slot], pa_r.at[slot])
+            group_recv(rb.at[slot], pa_r.at[slot], ranks - 1)
             tree_solve(slot)
             xr[slot, me] = xb[slot, me]
             for n in range(len(offsets)):
                 remote(
-                    xb.at[slot, peer(n)], xr.at[slot, me], xa_s.at[slot, n], xa_r.at[slot, me], rank_device(peer(n))
+                    xb.at[slot, peer(n)], xr.at[slot, me], xa_s.at[slot], xa_r.at[slot, me // NV], rank_device(peer(n))
                 ).start()
 
         def unmerge(step, carry):
-            for v in range(NV):
-                origin = step * NV + v
-
-                @pl.when(origin != me)
-                def _(origin=origin):
-                    remote(
-                        xr.at[slot, origin],
-                        xr.at[slot, origin],
-                        xa_r.at[slot, origin],
-                        xa_r.at[slot, origin],
-                        rank_device(origin),
-                    ).wait_recv()
+            @pl.when(me // NV == step)
+            def _():
+                group_recv(xr.at[slot], xa_r.at[slot, step], NV - 1)
+
+            @pl.when(me // NV != step)
+            def _():
+                group_recv(xr.at[slot], xa_r.at[slot, step], NV)
 
             a_cross, a_last, b_first, b_cross, d = (gm[1, step, n] for n in range(5))
             for v in range(NV):
@@ -581,7 +635,7 @@
     for copy in ax_halo:
         copy.wait_recv()
     q_halo = section(0)
-    for copy in q_halo + rad_halo + dt_halo:
+    for copy in q_halo:
         copy.wait_recv()
 
     def update_one(t, carry):
@@ -610,7 +664,7 @@
 
     def stores(t):
         return [
-            pltpu.make_async_copy(u2.at[:, i + 2, tile(t)], out.at[:, tile(t), i, :], out_sem.at[t, i])
+            pltpu.make_async_copy(u2.at[:, i + 2, tile(t)], out.at[:, tile(t), i, :], out_sem)
             for i in range(ROWS)
         ]
 
@@ -629,36 +683,9 @@
 
     lax.fori_loop(0, HALF, lambda step, carry: update_two(mine + step, carry), 0)
     lax.fori_loop(0, HALF, update_two_late, 0)
-
-    for copy in pending:
-        copy.wait_send()
-    spread_end(g_source, gt, ga_s, ga_r)
-
-    def sent(t, carry):
-        for copy in chunk_pair(t):
-            copy.wait_send()
-        return carry
-
-    lax.fori_loop(0, TILES, sent, 0)
-    for slot in range(2):
-        spread_end(lambda target, slot=slot: mb.at[slot, target], rb.at[slot], pa_s.at[slot], pa_r.at[slot])
-        for step in range(HALF):
-            pair_copy(slot, step).wait_send()
-            back_copy(slot, step).wait_send()
-
-        @pl.when(me < UNITS)
-        def _(slot=slot):
-            for n in range(len(offsets)):
-                remote(
-                    xb.at[slot, peer(n)], xr.at[slot, me], xa_s.at[slot, n], xa_r.at[slot, me], rank_device(peer(n))
-                ).wait_send()
-
-    def stored(t, carry):
-        for copy in stores(t):
-            copy.wait()
-        return carry
-
-    lax.fori_loop(0, TILES, stored, 0)
+    section_sent(1)
+
+    landed(u2.at[:, pl.ds(2, ROWS)], out_sem)
 
 
 def solution(mesh):
@@ -673,7 +700,6 @@
         dma = lambda *shape: pltpu.SemaphoreType.DMA(shape)
         plane = (layers, LANES)
         cell = (SUB, LANES)
-        peers = ranks - 1
         scratch = [
             vmem(NV, ROWS + 4, *plane),
             vmem(NV, ROWS + 4, *plane),
@@ -705,8 +731,8 @@
             vmem(2, HALF, NV, 2, *cell),
             vmem(3, NV, NV, *cell),
             vmem(2, NV, *cell),
-            dma(4, ROWS),
-            dma(TILES, ROWS),
+            dma(5),
+            pltpu.SemaphoreType.DMA,
             dma(2, TILES),
             dma(2, TILES),
             dma(2, 2),
@@ -717,16 +743,17 @@
             dma(2),
             pltpu.SemaphoreType.DMA,
             pltpu.SemaphoreType.DMA,
-            dma(UNITS),
-            dma(ranks),
+            pltpu.SemaphoreType.DMA,
+            pltpu.SemaphoreType.DMA,
             dma(2, HALF),
             dma(2, HALF),
-            dma(2, UNITS),
-            dma(2, ranks),
-            dma(2, peers),
-            dma(2, ranks),
+            dma(2),
+            dma(2),
+            dma(2),
             dma(2, HALF),
             dma(2, HALF),
+            dma(2, HALF),
+            pltpu.SemaphoreType.REGULAR((3,)),
         ]
         anywhere = pl.BlockSpec(memory_space=pl.ANY)
         scalars = pl.BlockSpec(memory_space=pltpu.SMEM)

time: 60.5 us -> 58.2 us (0.962)
  Pallas kernels: 58.1 us -> 55.8 us
    pallas_call x1, Pallas kernels: 58.1 us -> 55.8 us  [on_device(): pl.pallas_call(functools.partial(kernel, nz, na), out_shape=jax.ShapeDtyp...]
where the time goes in v2:
time: 58.2 us; the launch traced here: 58 us
  Pallas kernels  55.8 us (96%)
  local copies, waits for them, and re-layouts  2.21 us (4%)
    pallas_call x1, Pallas kernels, on_device(): pl.pallas_call(functools.partial(kernel, nz, na), out_shape=jax.ShapeDtyp...  55.8 us
    unnamed x1, local copies, waits for them, and re-layouts  2.21 us

profile of v2, /device:TPU:1, one launch (start us, length us, event | category | flops | bytes accessed | tf_op | source)
XLA Modules:
  0.0 58.0 jit_solution(6832689967097499747)
XLA Ops:
  0.0 55.8 %shard_map.64 = f32[5,48,8,128]{3,2,1,0:T(8,128)} custom-call(f32[5,48,8,128]{3,2,1,0:T(8,128)} %fields.1, f32[48,8,128]{2,1,0:T(8,128)} %inv_volume.1, f32[48,8,128]{2,1,0:T(8,128)} %radius_ratio.1, f32[48,8,128]{2,1,0:T(8,128)} %time_step.1, f32[5,5]{1,0:T(8,128)} %jac_c.1, f32[5,2,5]{2,1,0:T(2,128)} %bitcast.1), custom_call_target="tpu_custom_call" | custom-call | tf_op jit(solution)/shard_map/pallas_call | solution.py:760
  55.8 2.2 %copy.8 = f32[5,48,8,128]{3,2,1,0:T(8,128)} copy(f32[5,48,8,128]{3,2,1,0:T(8,128)} %shard_map.64) | data formatting | bytes 1966080

commit v3 on v2

--- a/solution.py
+++ b/solution.py
@@ -66,7 +66,6 @@
     tab,
     edge,
     in_sem,
-    out_sem,
     uc_s,
     uc_r,
     circ_s,
@@ -97,31 +96,35 @@
     me = z * 2 + y
 
     def blk_device(b):
-        return {"blk_0": b // 4, "blk_1": (b // 2) % 2, "blk_2": b % 2, "axial": a}
+        return {"blk_0": lax.div(b, 4), "blk_1": lax.rem(lax.div(b, 2), 2), "blk_2": lax.rem(b, 2), "axial": a}
 
     def ax_device(index):
         return {"blk_0": z, "blk_1": y, "blk_2": c, "axial": index}
 
     def rank_device(rank):
-        return {"blk_0": rank // 2, "blk_1": rank % 2, "blk_2": c, "axial": a}
+        if isinstance(rank, int):
+            return {"blk_0": rank // 2, "blk_1": rank % 2, "blk_2": c, "axial": a}
+        return {"blk_0": lax.div(rank, 2), "blk_1": lax.rem(rank, 2), "blk_2": c, "axial": a}
+
+    def plane_device(plane, column):
+        return {"blk_0": plane, "blk_1": column, "blk_2": c, "axial": a}
+
+    def around(value, count):
+        return lax.rem(value, count)
 
     b = me * 2 + c
     size = ranks * 2
-    right = blk_device((b + 1) % size)
-    left = blk_device((b + size - 1) % size)
-    ax_up = ax_device((a + 1) % na)
-    ax_down = ax_device((a + na - 1) % na)
+    right = blk_device(around(b + 1, size))
+    left = blk_device(around(b + size - 1, size))
+    ax_up = ax_device(around(a + 1, na))
+    ax_down = ax_device(around(a + na - 1, na))
     partner = {"blk_0": z, "blk_1": y, "blk_2": 1 - c, "axial": a}
     hops = [dz for k in range(nz // 2, 0, -1) for dz in dict.fromkeys((k, nz - k))] + [0]
     offsets = [(dz, dy) for dz in hops for dy in (1, 0) if (dz, dy) != (0, 0)]
 
     def peer(n):
         dz, dy = offsets[n]
-        return ((z + dz) % nz) * 2 + (y + dy) % 2
-
-    def source(n):
-        dz, dy = offsets[n]
-        return ((z + nz - dz) % nz) * 2 + (y + dy) % 2
+        return around(z + dz, nz), (1 - y if dy else y)
 
     def remote(src, dst, ssem, rsem, device):
         return pltpu.make_async_remote_copy(
@@ -144,7 +147,7 @@
         pltpu.make_async_copy(part, part, semaphore).wait()
 
     def beside(dz, dy):
-        return rank_device(((z + nz + dz) % nz) * 2 + (y + dy) % 2)
+        return plane_device(around(z + nz + dz, nz), 1 - y if dy else y)
 
     def signal(semaphore, device):
         pl.semaphore_signal(semaphore, inc=1, device_id=device, device_id_type=pl.DeviceIdType.MESH)
@@ -231,7 +234,7 @@
     mine = HALF * c
 
     def chunk_send(step, carry):
-        for copy in chunk_pair((step + mine) % TILES):
+        for copy in chunk_pair(around(step + mine, TILES)):
             copy.start()
         return carry
 
@@ -335,8 +338,8 @@
                 ROWS - 1: mix(0, [8.0 * q - p for p, q in zip(high2, high1)]),
             }
         near = (lane < 2) | (lane >= LANES - 2)
-        half = t // HALF
-        base = (t % HALF) * ROWS
+        half = lax.div(t, HALF)
+        base = lax.rem(t, HALF) * ROWS
         ahead = [jnp.zeros((SUB, LANES), F32)] * NV
         start = [jnp.zeros((SUB, LANES), F32)] * NV
         product = jnp.ones((SUB, LANES), F32)
@@ -586,7 +589,7 @@
         @pl.when(me < UNITS)
         def _():
             if slot == 0:
-                gt[me] = gm[0, me // NV, pl.ds(0, 3)]
+                gt[me] = gm[0, lax.div(me, NV), pl.ds(0, 3)]
                 group_recv(gt, ga_r, ranks - 1)
                 tree_factors()
             rb[slot, me] = mb[slot, me]
@@ -594,16 +597,21 @@
             tree_solve(slot)
             xr[slot, me] = xb[slot, me]
             for n in range(len(offsets)):
+                plane, column = peer(n)
                 remote(
-                    xb.at[slot, peer(n)], xr.at[slot, me], xa_s.at[slot], xa_r.at[slot, me // NV], rank_device(peer(n))
+                    xb.at[slot, plane * 2 + column],
+                    xr.at[slot, me],
+                    xa_s.at[slot],
+                    xa_r.at[slot, lax.div(me, NV)],
+                    plane_device(plane, column),
                 ).start()
 
         def unmerge(step, carry):
-            @pl.when(me // NV == step)
+            @pl.when(lax.div(me, NV) == step)
             def _():
                 group_recv(xr.at[slot], xa_r.at[slot, step], NV - 1)
 
-            @pl.when(me // NV != step)
+            @pl.when(lax.div(me, NV) != step)
             def _():
                 group_recv(xr.at[slot], xa_r.at[slot, step], NV)
 
@@ -662,19 +670,12 @@
         copy.wait_recv()
     section(1)
 
-    def stores(t):
-        return [
-            pltpu.make_async_copy(u2.at[:, i + 2, tile(t)], out.at[:, tile(t), i, :], out_sem)
-            for i in range(ROWS)
-        ]
-
     def update_two(t, carry):
         for v in range(NV):
             _, _, values = sweep(1, t, v)
             for i, value in enumerate(values):
-                u2[v, i + 2, tile(t)] = u1[v, i + 2, tile(t)] + dt[i + 2, tile(t)] * value
-        for copy in stores(t):
-            copy.start()
+                start = pl.multiple_of((v * TILES + t) * (SUB * ROWS), SUB) + i
+                out[pl.ds(start, SUB, stride=ROWS), :] = u1[v, i + 2, tile(t)] + dt[i + 2, tile(t)] * value
         return carry
 
     def update_two_late(step, carry):
@@ -684,8 +685,6 @@
     lax.fori_loop(0, HALF, lambda step, carry: update_two(mine + step, carry), 0)
     lax.fori_loop(0, HALF, update_two_late, 0)
     section_sent(1)
-
-    landed(u2.at[:, pl.ds(2, ROWS)], out_sem)
 
 
 def solution(mesh):
@@ -732,7 +731,6 @@
             vmem(3, NV, NV, *cell),
             vmem(2, NV, *cell),
             dma(5),
-            pltpu.SemaphoreType.DMA,
             dma(2, TILES),
             dma(2, TILES),
             dma(2, 2),
@@ -757,14 +755,19 @@
         ]
         anywhere = pl.BlockSpec(memory_space=pl.ANY)
         scalars = pl.BlockSpec(memory_space=pltpu.SMEM)
-        return pl.pallas_call(
+        rows = fields.shape[0] * layers * fields.shape[2]
+        operands = (fields, inv_volume, radius_ratio, time_step, jac_circ, jnp.transpose(jac_other, (1, 0, 2)))
+        result = pl.pallas_call(
             functools.partial(kernel, nz, na),
-            out_shape=jax.ShapeDtypeStruct(fields.shape, F32),
+            out_shape=jax.ShapeDtypeStruct((rows, LANES), F32),
             in_specs=[anywhere] * 4 + [scalars] * 2,
-            out_specs=anywhere,
+            out_specs=pl.BlockSpec(memory_space=pltpu.VMEM),
             scratch_shapes=scratch,
-            compiler_params=pltpu.CompilerParams(collective_id=0, has_side_effects=True),
-        )(fields, inv_volume, radius_ratio, time_step, jac_circ, jnp.transpose(jac_other, (1, 0, 2)))
+            compiler_params=pltpu.CompilerParams(
+                collective_id=0, has_side_effects=True, vmem_limit_bytes=24 * 1024 * 1024
+            ),
+        )(*(pltpu.with_memory_space_constraint(x, pltpu.HBM) for x in operands))
+        return result.reshape(fields.shape)
 
     return jax.shard_map(
         on_device,

time: 58.2 us -> 56.2 us (0.966)
  local copies, waits for them, and re-layouts: 2.21 us -> 0.95 us
  Pallas kernels: 55.8 us -> 55 us
    unnamed x1, local copies, waits for them, and re-layouts: 2.21 us -> 0.95 us
    pallas_call x1, Pallas kernels: 55.8 us -> 55 us  [on_device(): pl.pallas_call(functools.partial(kernel, nz, na), out_shape=jax.ShapeDtyp...]
where the time goes in v3:
time: 56.2 us; the launch traced here: 56 us
  Pallas kernels  55 us (98%)
  local copies, waits for them, and re-layouts  0.95 us (2%)
    pallas_call x1, Pallas kernels, on_device(): pl.pallas_call(functools.partial(kernel, nz, na), out_shape=jax.ShapeDtyp...  55 us

profile of v3, /device:TPU:1, one launch (start us, length us, event | category | flops | bytes accessed | tf_op | source)
XLA Modules:
  0.0 56.0 jit_solution(18208495089206248082)
XLA Ops:
  0.0 55.0 %shard_map.64 = f32[1920,128]{1,0:T(8,128)S(1)} custom-call(f32[5,48,8,128]{3,2,1,0:T(8,128)} %fields.1, f32[48,8,128]{2,1,0:T(8,128)} %inv_volume.1, f32[48,8,128]{2,1,0:T(8,128)} %radius_ratio.1, f32[48,8,128]{2,1,0:T(8,128)} %time_step.1, f32[5,5]{1,0:T(8,128)} %jac_c.1, f32[5,2,5]{2,1,0:T(2,128)} %bitcast.3), custom_call_target="tpu_custom_call" | custom-call | tf_op jit(solution)/shard_map/pallas_call | solution.py:760
  55.0 0.9 %copy.8 = f32[5,48,8,128]{3,2,1,0:T(8,128)} copy(f32[5,48,8,128]{3,2,1,0:T(8,128)S(1)} %bitcast.2) | data formatting | bytes 1966080

commit v4 on v3

--- a/solution.py
+++ b/solution.py
@@ -153,10 +153,12 @@
         pl.semaphore_signal(semaphore, inc=1, device_id=device, device_id_type=pl.DeviceIdType.MESH)
 
     barrier = pltpu.get_barrier_semaphore()
-    greet = [ax_up, ax_down, right, left, beside(1, 1), beside(-1, 1), beside(1, 0), beside(-1, 0), beside(0, 1), partner]
+    greet = [right, left, beside(1, 1), beside(-1, 1), beside(1, 0), beside(-1, 0), beside(0, 1), partner]
     edge_rows, inner_rows = (0, 1, ROWS - 2, ROWS - 1), range(2, ROWS - 2)
     for i in edge_rows:
         load_u(i, 0)
+    pl.when(a < na - 1)(lambda: signal(barrier, ax_up))
+    pl.when(a > 0)(lambda: signal(barrier, ax_down))
     for device in greet:
         signal(barrier, device)
     for i in inner_rows:
@@ -198,7 +200,7 @@
     blank = (jnp.zeros((SUB, LANES), F32),) * (2 * NV)
 
     landed(u1.at[:, pl.ds(2, len(edge_rows))], in_sem.at[0])
-    pl.semaphore_wait(barrier, len(greet))
+    pl.semaphore_wait(barrier, len(greet) + jnp.minimum(a, 1) + jnp.minimum(na - 1 - a, 1))
 
     def circ_pair(ref, which, low, width):
         def part(start):
@@ -223,6 +225,26 @@
         return [to_left, to_right]
 
     pending = []
+    axial_pending = []
+
+    class Axial:
+        def __init__(self, pair):
+            self.up, self.down = pair
+
+        def start(self):
+            pl.when(a < na - 1)(self.up.start)
+            pl.when(a > 0)(self.down.start)
+            axial_pending.append(self)
+            return self
+
+        def wait_recv(self):
+            pl.when(a > 0)(self.up.wait_recv)
+            pl.when(a < na - 1)(self.down.wait_recv)
+
+        def wait_send(self):
+            pl.when(a < na - 1)(self.up.wait_send)
+            pl.when(a > 0)(self.down.wait_send)
+
 
     def begin(copies):
         for copy in copies:
@@ -244,7 +266,18 @@
     load_cell(inv_volume, vol, 0, 3)
     landed(u1.at[:, pl.ds(2, len(inner_rows))], in_sem.at[1])
     keep_packed(0, lax.fori_loop(0, TILES, functools.partial(pack, u1), blank))
-    ax_halo = begin(axial_pair(0))
+    ax_halo = Axial(axial_pair(0)).start()
+
+    @pl.when(a == 0)
+    def _():
+        for slot in range(2):
+            pkh[slot, 0] = jnp.zeros((NV, SUB, LANES), F32)
+
+    @pl.when(a == na - 1)
+    def _():
+        for slot in range(2):
+            pkh[slot, 1] = jnp.zeros((NV, SUB, LANES), F32)
+
     for v in range(NV):
         for m in range(NV):
             tab[0, v, m] = jnp.broadcast_to(jac_c[v, m] / 12.0, (SUB, LANES))
@@ -531,6 +564,9 @@
         for copy in pending:
             copy.wait_send()
         pending.clear()
+        for copy in axial_pending:
+            copy.wait_send()
+        axial_pending.clear()
         spread_end(gt, ga_s)
 
         def sent(t, carry):
@@ -640,8 +676,7 @@
             values[i] = later
         return low, high, values
 
-    for copy in ax_halo:
-        copy.wait_recv()
+    ax_halo.wait_recv()
     q_halo = section(0)
     for copy in q_halo:
         copy.wait_recv()
@@ -664,10 +699,9 @@
     packed = lax.fori_loop(0, HALF, lambda step, carry: update_one(mine + step, carry), blank)
     packed = lax.fori_loop(0, HALF, update_one_late, packed)
     keep_packed(1, packed)
-    ax_halo = begin(axial_pair(1))
+    ax_halo = Axial(axial_pair(1)).start()
     lax.fori_loop(0, TILES, functools.partial(local_step, u2, 1), 0)
-    for copy in ax_halo:
-        copy.wait_recv()
+    ax_halo.wait_recv()
     section(1)
 
     def update_two(t, carry):

time: 56.2 us -> 54 us (0.961)
  Pallas kernels: 55 us -> 52.8 us
    pallas_call x1, Pallas kernels: 55 us -> 52.8 us  [on_device(): pl.pallas_call(functools.partial(kernel, nz, na), out_shape=jax.ShapeDtyp...]
where the time goes in v4:
time: 54 us; the launch traced here: 53.8 us
  Pallas kernels  52.8 us (98%)
  local copies, waits for them, and re-layouts  0.95 us (2%)
    pallas_call x1, Pallas kernels, on_device(): pl.pallas_call(functools.partial(kernel, nz, na), out_shape=jax.ShapeDtyp...  52.8 us

profile of v4, /device:TPU:1, one launch (start us, length us, event | category | flops | bytes accessed | tf_op | source)
XLA Modules:
  0.0 53.8 jit_solution(1179266829758313015)
XLA Ops:
  0.0 52.8 %shard_map.64 = f32[1920,128]{1,0:T(8,128)S(1)} custom-call(f32[5,48,8,128]{3,2,1,0:T(8,128)} %fields.1, f32[48,8,128]{2,1,0:T(8,128)} %inv_volume.1, f32[48,8,128]{2,1,0:T(8,128)} %radius_ratio.1, f32[48,8,128]{2,1,0:T(8,128)} %time_step.1, f32[5,5]{1,0:T(8,128)} %jac_c.1, f32[5,2,5]{2,1,0:T(2,128)} %bitcast.3), custom_call_target="tpu_custom_call" | custom-call | tf_op jit(solution)/shard_map/pallas_call | solution.py:794
  52.9 0.9 %copy.8 = f32[5,48,8,128]{3,2,1,0:T(8,128)} copy(f32[5,48,8,128]{3,2,1,0:T(8,128)S(1)} %bitcast.2) | data formatting | bytes 1966080
